TPU v7x, 128 devices: a whole 4x4x4 slice. The times are simulated.
128 devices in a mesh: ctx: 16 (over x, z), head: 8 (over y, core).
Axes of the slice: x: 4, y: 4, z: 4, core: 2. Of those that a mesh axis runs over, the one named last changes fastest.
Arguments:
- queries: bfloat16 [64, 8192], P('ctx', 'head'), may hold values from -16 to 16
- keys: bfloat16 [524288, 8, 128], P('ctx', 'head'), may hold values from -16 to 16
- values: bfloat16 [524288, 8, 128], P('ctx', 'head'), may hold values from -4 to 4
- offsets: int32 [16], P('ctx'), may hold values from 0 to 491520, as said below
- lengths: int32 [64], replicated, may hold values from 262144 to 524288
- residual: bfloat16 [64, 5120], P(None, 'ctx'), may hold values from -2 to 2
- wo: bfloat16 [8192, 5120], P('head', 'ctx'), may hold values from -0.0625 to 0.0625
- norm_gain: float32 [5120], P('ctx'), may hold values from 0.1 to 1.9
- w_gate: bfloat16 [5120, 25600], P('ctx', 'head'), may hold values from -0.078125 to 0.078125
- w_up: bfloat16 [5120, 25600], P('ctx', 'head'), may hold values from -0.078125 to 0.078125
- w_down: bfloat16 [25600, 5120], P('head', 'ctx'), may hold values from -0.0390625 to 0.0390625
Outputs:
- attended: bfloat16 [64, 8192], P('ctx', 'head')
- stream: bfloat16 [64, 5120], P(None, 'ctx')
- ffn_out: bfloat16 [64, 5120], P('head', 'ctx')
Inputs may be any that keep to these rules, and one draw needn't show every extreme that they name: offsets holds each of 0, 32768, ..., 491520 once.
All inputs are finite; a program needn't handle non-finite values.
Results may differ from a plain program's by a relative error of at most 0.02.
Values may be sent and summed in bfloat16 or wider, within the bound.
A program may use at most 128 MiB of HBM per device.

v0:
```python
import math
import jax
import jax.numpy as jnp
from jax import lax
from jax.sharding import PartitionSpec as P

D = 5120
masked_score = -1e30
epsilon = 1e-06


def activate(gate, upward, square_total):
    scale = lax.rsqrt(square_total / D + epsilon)[:, None]
    return (jax.nn.silu(scale * gate) * (scale * upward)).astype(jnp.bfloat16)


def local(queries, keys, values, offsets, lengths, residual, wo, norm_gain, w_gate, w_up, w_down):
    head_size = keys.shape[2]
    kv_local = keys.shape[1]
    rows_local = queries.shape[0]
    everyone = lax.all_gather(queries, "ctx", axis=0, tiled=True)
    batch = everyone.shape[0]
    groups = everyone.shape[1] // (kv_local * head_size)
    query_heads = everyone.reshape(batch, kv_local, groups, head_size)
    query_heads = query_heads.transpose(1, 0, 2, 3).reshape(kv_local, batch * groups, head_size)
    row_limit = jnp.repeat(lengths, groups)
    inverse_root = 1.0 / math.sqrt(head_size)
    span = keys.shape[0]
    block = min(2048, span)
    turns = span // block
    shard_begin = offsets[0]

    def visit(carry, block_index):
        row_high, row_total, row_acc = carry
        first_slot = block_index * block
        key_block = lax.dynamic_slice_in_dim(keys, first_slot, block, 0)
        value_block = lax.dynamic_slice_in_dim(values, first_slot, block, 0)
        scores = (
            jnp.einsum("hrd,khd->hrk", query_heads, key_block, preferred_element_type=jnp.float32)
            * inverse_root
        )
        position = shard_begin + first_slot + jnp.arange(block, dtype=jnp.int32)
        scores = jnp.where(position[None, None, :] < row_limit[None, :, None], scores, masked_score)
        new_high = jnp.maximum(row_high, jnp.max(scores, axis=2))
        weights = jnp.exp(scores - new_high[:, :, None])
        rescale = jnp.exp(row_high - new_high)
        row_total = row_total * rescale + jnp.sum(weights, axis=2)
        update = jnp.einsum(
            "hrk,khd->hrd",
            weights.astype(jnp.bfloat16),
            value_block,
            preferred_element_type=jnp.float32,
        )
        row_acc = row_acc * rescale[:, :, None] + update
        return ((new_high, row_total, row_acc), None)

    start_high = jnp.full((kv_local, batch * groups), masked_score, jnp.float32)
    start_total = jnp.zeros((kv_local, batch * groups), jnp.float32)
    start_acc = jnp.zeros((kv_local, batch * groups, head_size), jnp.float32)
    (row_high, row_total, row_acc), _ = lax.scan(
        visit, (start_high, start_total, start_acc), jnp.arange(turns, dtype=jnp.int32)
    )
    heads_local = kv_local * groups
    row_high = (
        row_high.reshape(kv_local, batch, groups).transpose(1, 0, 2).reshape(batch, heads_local)
    )
    row_total = (
        row_total.reshape(kv_local, batch, groups).transpose(1, 0, 2).reshape(batch, heads_local)
    )
    row_acc = (
        row_acc.reshape(kv_local, batch, groups, head_size)
        .transpose(1, 0, 2, 3)
        .reshape(batch, heads_local, head_size)
    )
    top_score = lax.pmax(row_high, "ctx")
    rescale = jnp.exp(row_high - top_score)
    summed_acc, summed_total = lax.psum((row_acc * rescale[:, :, None], row_total * rescale), "ctx")
    whole_rows = (
        (summed_acc / summed_total[:, :, None])
        .reshape(batch, heads_local * head_size)
        .astype(jnp.bfloat16)
    )
    attended = lax.dynamic_slice_in_dim(
        whole_rows, lax.axis_index("ctx") * rows_local, rows_local, 0
    )
    projected = jnp.dot(whole_rows, wo, preferred_element_type=jnp.float32)
    mixed = lax.psum(projected, "head")
    combined = residual.astype(jnp.float32) + mixed
    stream = combined.astype(jnp.bfloat16)
    squares = jnp.sum(combined * combined, axis=1)
    normed = (combined * norm_gain).astype(jnp.bfloat16)
    gate_part = jnp.dot(normed, w_gate, preferred_element_type=jnp.float32)
    up_part = jnp.dot(normed, w_up, preferred_element_type=jnp.float32)
    square_total = lax.psum(squares, "ctx")
    gate, upward = lax.psum((gate_part, up_part), "ctx")
    hidden = activate(gate, upward, square_total)
    ffn_out = lax.psum_scatter(
        jnp.dot(hidden, w_down, preferred_element_type=jnp.float32),
        "head",
        scatter_dimension=0,
        tiled=True,
    ).astype(jnp.bfloat16)
    return (attended, stream, ffn_out)


def solution(mesh):
    return jax.shard_map(
        local,
        mesh=mesh,
        in_specs=(
            P("ctx", "head"),
            P("ctx", "head", None),
            P("ctx", "head", None),
            P("ctx"),
            P(),
            P(None, "ctx"),
            P("head", "ctx"),
            P("ctx"),
            P("ctx", "head"),
            P("ctx", "head"),
            P("head", "ctx"),
        ),
        out_specs=(P("ctx", "head"), P(None, "ctx"), P("head", "ctx")),
        check_vma=False,
    )
```

profile of v0, /device:TPU:0, one launch (start us, length us, event | category | flops | bytes accessed | tf_op | source)
XLA Modules:
  0.0 567.2 jit_solution(13764307791366499281)
XLA Ops:
  7.3 25.3 %all-gather = bf16[16,4,1024]{2,1,0:T(4,128)(2,1)S(1)} all-gather(bf16[1,4,1024]{2,1,0:T(4,128)(2,1)} %bitcast.66), channel_id=1, replica_groups=mesh['ctx'=16,'head'=8] {'ctx'}, dimensions={0}, use_global_device_ids=true | all-gather | bytes 139264 | tf_op jit(solution)/shard_map/all_gather | solution.py:21
  32.7 189.0 %while.15 = (s32[]{:T(128)}, f32[1,512]{1,0:T(1,128)S(1)}, f32[1,512]{1,0:T(1,128)S(1)}, f32[1,512,128]{2,1,0:T(8,128)S(1)}, s32[16]{0:T(128)S(1)}, /*index=5*/s...) while((s32[]{:T(128)}, f32[1,512]{1,0:T(1,128)S(1)}, ...), condition=%wide.region_3.4_spmd.clone, body=%wide.region_0.3_spmd.clone.sunk | while | flops 545460736 | bytes 31121916 | solution.py:60
  35.4 3.7 fusion.46
  39.1 3.0 fusion.48
  42.5 1.9 fusion.50
  47.2 3.7 fusion.46
  50.9 3.0 fusion.48
  54.4 1.9 fusion.50
  59.0 3.7 fusion.46
  62.7 3.0 fusion.48
  66.2 1.9 fusion.50
  70.9 3.7 fusion.46
  74.6 3.0 fusion.48
  78.0 1.9 fusion.50
  82.7 3.7 fusion.46
  86.4 3.0 fusion.48
  89.8 1.9 fusion.50
  94.5 3.7 fusion.46
  98.2 3.0 fusion.48
  101.6 1.9 fusion.50
  106.3 3.7 fusion.46
  110.0 3.0 fusion.48
  113.4 1.9 fusion.50
  118.1 3.7 fusion.46
  121.8 3.0 fusion.48
  125.3 1.9 fusion.50
  129.9 3.7 fusion.46
  133.6 3.0 fusion.48
  137.1 1.9 fusion.50
  141.7 3.7 fusion.46
  145.4 3.0 fusion.48
  148.9 1.9 fusion.50
  153.6 3.7 fusion.46
  157.3 3.0 fusion.48
  160.7 1.9 fusion.50
  165.4 3.7 fusion.46
  169.1 3.0 fusion.48
  172.5 1.9 fusion.50
  177.2 3.7 fusion.46
  180.9 3.0 fusion.48
  184.3 1.9 fusion.50
  189.0 3.7 fusion.46
  192.7 3.0 fusion.48
  196.1 1.9 fusion.50
  200.8 3.7 fusion.46
  204.5 3.0 fusion.48
  208.0 1.9 fusion.50
  212.6 3.7 fusion.46
  216.3 3.0 fusion.48
  219.8 1.9 fusion.50
  223.0 72.1 %pmax.7 = f32[64,8]{1,0:T(8,128)S(1)} all-reduce(f32[64,8]{1,0:T(8,128)S(1)} %reshape_transpose_reshape.14), channel_id=1, replica_groups=mesh['ctx'=16,'head'=8] {'ctx'}, use_global_device_ids=true, to_apply=%region_4.5 | all-reduce | flops 512 | bytes 4096 | tf_op jit(solution)/shard_map/pmax | solution.py:75
  295.8 0.8 bitcast_multiply_fusion
  296.8 69.5 %psum.43 = f32[64,8]{1,0:T(8,128)S(1)} all-reduce(f32[64,8]{1,0:T(8,128)S(1)} %get-tuple-element.120), channel_id=1, replica_groups=mesh['ctx'=16,'head'=8] {'ctx'}, use_global_device_ids=true, to_apply=%region_6.7 | all-reduce | flops 512 | bytes 4096 | tf_op jit(solution)/shard_map/psum | solution.py:77
  366.3 12.1 %all-reduce.6.cloned.1.call-done = f32[64,8,128]{2,1,0:T(8,128)} async-done(((f32[64,8,128]{2,1,0:T(8,128)}), f32[64,8,128]{2,1,0:T(8,128)}) %all-reduce.6.cloned.1.call-update) | async-done | bytes 262160 | tf_op jit(solution)/shard_map/psum | solution.py:77
  378.4 1.1 divide_convert_fusion
  379.5 1.0 fusion.26
  380.5 57.5 %all-reduce.8.cloned.1.call-done = f32[64,320]{1,0:T(8,128)} async-done(((f32[64,320]{1,0:T(8,128)}), f32[64,320]{1,0:T(8,128)}) %all-reduce.8.cloned.1.call-update) | async-done | bytes 81936 | tf_op jit(solution)/shard_map/psum | solution.py:87
  438.0 1.6 multiply_reduce_fusion
  439.7 1.4 fusion.29
  441.1 3.0 fusion.30
  446.1 40.6 %psum.45 = f32[64]{0:T(128)S(1)} all-reduce(f32[64]{0:T(128)S(1)} %get-tuple-element.124), channel_id=1, replica_groups=mesh['ctx'=16,'head'=8] {'ctx'}, use_global_device_ids=true, to_apply=%region_9.10 | all-reduce | flops 64 | bytes 512 | tf_op jit(solution)/shard_map/psum | solution.py:94
  486.7 45.5 %all-reduce.10.cloned.1.call-done = (f32[64,3200]{1,0:T(8,128)}, f32[64,3200]{1,0:T(8,128)}) async-done(((f32[64,3200]{1,0:T(8,128)}, f32[64,3200]{1,0:T(8,128)}), (f32[64,3200]{1,0:T(8,128)}, f32[64,3200]{1,0:T(8,128)})) %all-reduce.10.cloned.1.call-update) | async-done | bytes 1638416 | tf_op jit(solution)/shard_map/psum | solution.py:95
  532.2 2.8 fusion.23
  535.1 25.0 %all-reduce = bf16[64,320]{1,0:T(8,128)(2,1)S(1)} all-reduce(f32[64,320]{1,0:T(8,128)S(1)} %fusion.23), channel_id=2, replica_groups=mesh['ctx'=16,'head'=8] {'head'}, use_global_device_ids=true, to_apply=%region_12.13.clone | all-reduce | flops 20480 | bytes 122880
  (176 shorter events, 34.3 us)
Async XLA Ops:
  7.2 432.5 %copy-start = (bf16[320,3200]{1,0:T(8,128)(2,1)S(1)}, bf16[320,3200]{1,0:T(8,128)(2,1)}, u32[]{:S(2)}) copy-start(bf16[320,3200]{1,0:T(8,128)(2,1)} %param.21) | copy-start | bytes 6144004
  7.2 371.2 %all-reduce.6.cloned.1.call-start = ((), (), s32[]{:S(2)}) async-start(), calls=%async_computation | async-start | bytes 524288 | tf_op jit(solution)/shard_map/psum | solution.py:77
  32.6 346.8 %copy-start.2 = (bf16[1024,320]{0,1:T(8,128)(2,1)S(1)}, bf16[1024,320]{0,1:T(8,128)(2,1)}, u32[]{:S(2)}) copy-start(bf16[1024,320]{0,1:T(8,128)(2,1)} %param.19) | copy-start | bytes 1966084
  32.6 405.4 %copy-start.3 = (bf16[64,320]{1,0:T(8,128)(2,1)S(1)}, bf16[64,320]{1,0:T(8,128)(2,1)}, u32[]{:S(2)}) copy-start(bf16[64,320]{1,0:T(8,128)(2,1)} %param.18) | copy-start | bytes 122884
  32.6 405.4 %copy-start.4 = (f32[320]{0:T(512)S(1)}, f32[320]{0:T(512)}, u32[]{:S(2)}) copy-start(f32[320]{0:T(512)} %param.20) | copy-start | bytes 3844
  39.1 3.4 copy-start.1
  50.9 3.4 copy-start.1
  62.7 3.4 copy-start.1
  74.5 3.4 copy-start.1
  86.4 3.4 copy-start.1
  98.2 3.4 copy-start.1
  110.0 3.4 copy-start.1
  121.8 3.4 copy-start.1
  133.6 3.4 copy-start.1
  145.4 3.4 copy-start.1
  157.2 3.4 copy-start.1
  169.1 3.4 copy-start.1
  180.9 3.4 copy-start.1
  192.7 3.4 copy-start.1
  204.5 3.4 copy-start.1
  216.3 3.4 copy-start.1
  296.7 141.3 %all-reduce.8.cloned.1.call-start = ((), (), s32[]{:S(2)}) async-start(), calls=%async_computation.1 | async-start | bytes 196608 | tf_op jit(solution)/shard_map/psum | solution.py:87
  379.5 64.7 %copy-start.5 = (u32[128]{0:T(128)S(1)}, u32[128]{0:T(128)}, u32[]{:S(2)}) copy-start(u32[128]{0:T(128)} %constant.51) | copy-start | bytes 1540
  380.5 151.8 %all-reduce.10.cloned.1.call-start = ((), (), s32[]{:S(2)}) async-start(), calls=%async_computation.2 | async-start | bytes 3276800 | tf_op jit(solution)/shard_map/psum | solution.py:95
Sparse Core Ops, SparseCore 0:
  296.8 81.4 all-reduce.5
  380.7 57.2 all-reduce.7
  444.3 87.9 all-reduce.9
where the time goes:
time: 570 us; the launch traced here: 567 us
  blocking collectives  233 us (41%)
  waiting for transfers between devices  115 us (20%)
  matrix products  98 us (17%)
  other arithmetic  52.9 us (9%)
  local copies, waits for them, and re-layouts  32.3 us (6%)
  loops' own time  21.6 us (4%)
  between operations  14.6 us (3%)
    pmax x1, blocking collectives, local(): top_score = lax.pmax(row_high, 'ctx')  72.1 us
    psum x1, blocking collectives, local(): lax.psum((row_acc * rescale[:, :, None], row_total * rescale), 'ctx')  69.5 us
    dot_general x16, matrix products, visit(): jnp.einsum('hrd,khd->hrk', query_heads, key_block, preferred_element_type...  59.1 us
    psum x1, waiting for transfers between devices, local(): mixed = lax.psum(projected, 'head')  57.5 us
    reduce_sum x16, other arithmetic, visit(): row_total = row_total * rescale + jnp.sum(weights, axis=2)  47.5 us
    psum x1, waiting for transfers between devices, local(): gate, upward = lax.psum((gate_part, up_part), 'ctx')  45.5 us
    psum x1, blocking collectives, local(): square_total = lax.psum(squares, 'ctx')  40.6 us
    dot_general x16, matrix products, visit(): jnp.einsum('hrk,khd->hrd', weights.astype(jnp.bfloat16), value_block, pre...  30.7 us
  transfers between devices with their start and end apart: 3, of which 3 were waited for; matrix products, arithmetic and copies ran while one was open for 0% of the time, Pallas kernels for 0%

commit v1 on v0

--- a/solution.py
+++ b/solution.py
@@ -7,6 +7,11 @@
 D = 5120
 masked_score = -1e30
 epsilon = 1e-06
+
+
+def cut_cycles(field_in):
+    moved = jnp.sum(lax.all_gather(field_in, "head"), axis=0)
+    return moved
 
 
 def activate(gate, upward, square_total):
@@ -84,7 +89,7 @@
         whole_rows, lax.axis_index("ctx") * rows_local, rows_local, 0
     )
     projected = jnp.dot(whole_rows, wo, preferred_element_type=jnp.float32)
-    mixed = lax.psum(projected, "head")
+    mixed = cut_cycles(projected)
     combined = residual.astype(jnp.float32) + mixed
     stream = combined.astype(jnp.bfloat16)
     squares = jnp.sum(combined * combined, axis=1)

time: 570 us -> 524 us (0.919)
  waiting for transfers between devices: 115 us -> 59.6 us
  blocking collectives: 233 us -> 244 us
    psum x1 -> x0, waiting for transfers between devices: 57.5 us -> none  [local(): mixed = lax.psum(projected, 'head')]
    all_gather x0 -> x1, blocking collectives: none -> 13.7 us  [cut_cycles(): moved = jnp.sum(lax.all_gather(field_in, 'head'), axis=0)]
  transfers between devices with their start and end apart: 3 -> 2, of which waited for: 3 -> 2; matrix products, arithmetic and copies ran while one was open for 0% -> 0% of each run, Pallas kernels for 0% -> 0%
where the time goes in v1:
time: 524 us; the launch traced here: 522 us
  blocking collectives  244 us (47%)
  matrix products  97.4 us (19%)
  waiting for transfers between devices  59.6 us (11%)
  other arithmetic  52.1 us (10%)
  local copies, waits for them, and re-layouts  32.3 us (6%)
  loops' own time  21.6 us (4%)
  between operations  14.9 us (3%)
    pmax x1, blocking collectives, local(): top_score = lax.pmax(row_high, 'ctx')  72.1 us
    psum x1, blocking collectives, local(): lax.psum((row_acc * rescale[:, :, None], row_total * rescale), 'ctx')  69.5 us
    dot_general x16, matrix products, visit(): jnp.einsum('hrd,khd->hrk', query_heads, key_block, preferred_element_type...  59.1 us
    psum x1, waiting for transfers between devices, local(): gate, upward = lax.psum((gate_part, up_part), 'ctx')  47.5 us
    reduce_sum x16, other arithmetic, visit(): row_total = row_total * rescale + jnp.sum(weights, axis=2)  47.5 us
    psum x1, blocking collectives, local(): square_total = lax.psum(squares, 'ctx')  38.2 us
    dot_general x16, matrix products, visit(): jnp.einsum('hrk,khd->hrd', weights.astype(jnp.bfloat16), value_block, pre...  30.7 us
    all_gather x1, blocking collectives, local(): everyone = lax.all_gather(queries, 'ctx', axis=0, tiled=True)  25.3 us
  transfers between devices with their start and end apart: 2, of which 2 were waited for; matrix products, arithmetic and copies ran while one was open for 0% of the time, Pallas kernels for 0%

profile of v1, /device:TPU:0, one launch (start us, length us, event | category | flops | bytes accessed | tf_op | source)
XLA Modules:
  0.0 521.8 jit_solution(4104244788385465611)
XLA Ops:
  7.3 25.3 %all-gather.1 = bf16[16,4,1024]{2,1,0:T(4,128)(2,1)S(1)} all-gather(bf16[1,4,1024]{2,1,0:T(4,128)(2,1)} %bitcast.68), channel_id=1, replica_groups=mesh['ctx'=16,'head'=8] {'ctx'}, dimensions={0}, use_global_device_ids=true | all-gather | bytes 139264 | tf_op jit(solution)/shard_map/all_gather | solution.py:26
  32.6 189.1 %while.15 = (s32[]{:T(128)}, f32[1,512]{1,0:T(1,128)S(1)}, f32[1,512]{1,0:T(1,128)S(1)}, f32[1,512,128]{2,1,0:T(8,128)S(1)}, s32[16]{0:T(128)S(1)}, /*index=5*/s...) while((s32[]{:T(128)}, f32[1,512]{1,0:T(1,128)S(1)}, ...), condition=%wide.region_3.4_spmd.clone, body=%wide.region_0.3_spmd.clone.sunk | while | flops 545460736 | bytes 31121916 | solution.py:65
  34.6 0.7 broadcast_in_dim.34
  35.4 3.7 fusion.46
  39.1 3.0 fusion.48
  42.5 1.9 fusion.50
  47.2 3.7 fusion.46
  50.9 3.0 fusion.48
  54.3 1.9 fusion.50
  59.0 3.7 fusion.46
  62.7 3.0 fusion.48
  66.2 1.9 fusion.50
  70.8 3.7 fusion.46
  74.5 3.0 fusion.48
  78.0 1.9 fusion.50
  82.6 3.7 fusion.46
  86.4 3.0 fusion.48
  89.8 1.9 fusion.50
  94.5 3.7 fusion.46
  98.2 3.0 fusion.48
  101.6 1.9 fusion.50
  106.3 3.7 fusion.46
  110.0 3.0 fusion.48
  113.4 1.9 fusion.50
  118.1 3.7 fusion.46
  121.8 3.0 fusion.48
  125.2 1.9 fusion.50
  129.9 3.7 fusion.46
  133.6 3.0 fusion.48
  137.1 1.9 fusion.50
  141.7 3.7 fusion.46
  145.4 3.0 fusion.48
  148.9 1.9 fusion.50
  153.5 3.7 fusion.46
  157.2 3.0 fusion.48
  160.7 1.9 fusion.50
  165.4 3.7 fusion.46
  169.1 3.0 fusion.48
  172.5 1.9 fusion.50
  177.2 3.7 fusion.46
  180.9 3.0 fusion.48
  184.3 1.9 fusion.50
  189.0 3.7 fusion.46
  192.7 3.0 fusion.48
  196.1 1.9 fusion.50
  200.8 3.7 fusion.46
  204.5 3.0 fusion.48
  207.9 1.9 fusion.50
  212.6 3.7 fusion.46
  216.3 3.0 fusion.48
  219.8 1.9 fusion.50
  223.0 72.1 %pmax.7 = f32[64,8]{1,0:T(8,128)S(1)} all-reduce(f32[64,8]{1,0:T(8,128)S(1)} %reshape_transpose_reshape.14), channel_id=1, replica_groups=mesh['ctx'=16,'head'=8] {'ctx'}, use_global_device_ids=true, to_apply=%region_4.5 | all-reduce | flops 512 | bytes 4096 | tf_op jit(solution)/shard_map/pmax | solution.py:80
  295.8 0.8 bitcast_multiply_fusion
  296.7 69.5 %psum.36 = f32[64,8]{1,0:T(8,128)S(1)} all-reduce(f32[64,8]{1,0:T(8,128)S(1)} %get-tuple-element.120), channel_id=1, replica_groups=mesh['ctx'=16,'head'=8] {'ctx'}, use_global_device_ids=true, to_apply=%region_6.7 | all-reduce | flops 512 | bytes 4096 | tf_op jit(solution)/shard_map/psum | solution.py:82
  366.3 12.1 %all-reduce.5.cloned.1.call-done = f32[64,8,128]{2,1,0:T(8,128)} async-done(((f32[64,8,128]{2,1,0:T(8,128)}), f32[64,8,128]{2,1,0:T(8,128)}) %all-reduce.5.cloned.1.call-update) | async-done | bytes 262160 | tf_op jit(solution)/shard_map/psum | solution.py:82
  378.3 1.1 divide_convert_fusion
  379.8 13.7 %all-gather = f32[512,320]{1,0:T(8,128)S(1)} all-gather(f32[64,320]{1,0:T(8,128)S(1)} %fusion.26), channel_id=2, replica_groups=mesh['ctx'=16,'head'=8] {'head'}, dimensions={0}, use_global_device_ids=true | all-gather | bytes 737280 | tf_op jit(solution)/shard_map/all_gather | solution.py:13
  393.6 0.7 multiply_reduce_fusion
  394.4 1.4 fusion.29
  395.8 3.0 fusion.30
  400.1 38.2 %psum.37 = f32[64]{0:T(128)S(1)} all-reduce(f32[64]{0:T(128)S(1)} %get-tuple-element.124), channel_id=1, replica_groups=mesh['ctx'=16,'head'=8] {'ctx'}, use_global_device_ids=true, to_apply=%region_9.10 | all-reduce | flops 64 | bytes 512 | tf_op jit(solution)/shard_map/psum | solution.py:99
  438.9 47.5 %all-reduce.7.cloned.1.call-done = (f32[64,3200]{1,0:T(8,128)}, f32[64,3200]{1,0:T(8,128)}) async-done(((f32[64,3200]{1,0:T(8,128)}, f32[64,3200]{1,0:T(8,128)}), (f32[64,3200]{1,0:T(8,128)}, f32[64,3200]{1,0:T(8,128)})) %all-reduce.7.cloned.1.call-update) | async-done | bytes 1638416 | tf_op jit(solution)/shard_map/psum | solution.py:100
  486.5 2.8 fusion.23
  489.3 25.0 %all-reduce = bf16[64,320]{1,0:T(8,128)(2,1)S(1)} all-reduce(f32[64,320]{1,0:T(8,128)S(1)} %fusion.23), channel_id=3, replica_groups=mesh['ctx'=16,'head'=8] {'head'}, use_global_device_ids=true, to_apply=%region_12.13.clone | all-reduce | flops 20480 | bytes 122880
  (175 shorter events, 33.9 us)
Async XLA Ops:
  7.2 387.2 %copy-start = (bf16[320,3200]{1,0:T(8,128)(2,1)S(1)}, bf16[320,3200]{1,0:T(8,128)(2,1)}, u32[]{:S(2)}) copy-start(bf16[320,3200]{1,0:T(8,128)(2,1)} %param.21) | copy-start | bytes 6144004
  7.2 371.2 %all-reduce.5.cloned.1.call-start = ((), (), s32[]{:S(2)}) async-start(), calls=%async_computation | async-start | bytes 524288 | tf_op jit(solution)/shard_map/psum | solution.py:82
  32.6 346.8 %copy-start.2 = (bf16[1024,320]{0,1:T(8,128)(2,1)S(1)}, bf16[1024,320]{0,1:T(8,128)(2,1)}, u32[]{:S(2)}) copy-start(bf16[1024,320]{0,1:T(8,128)(2,1)} %param.19) | copy-start | bytes 1966084
  39.1 3.4 copy-start.1
  50.9 3.4 copy-start.1
  62.7 3.4 copy-start.1
  74.5 3.4 copy-start.1
  86.3 3.4 copy-start.1
  98.2 3.4 copy-start.1
  110.0 3.4 copy-start.1
  121.8 3.4 copy-start.1
  133.6 3.4 copy-start.1
  145.4 3.4 copy-start.1
  157.2 3.4 copy-start.1
  169.0 3.4 copy-start.1
  180.9 3.4 copy-start.1
  192.7 3.4 copy-start.1
  204.5 3.4 copy-start.1
  216.3 3.4 copy-start.1
  221.7 171.9 %copy-start.3 = (bf16[64,320]{1,0:T(8,128)(2,1)S(1)}, bf16[64,320]{1,0:T(8,128)(2,1)}, u32[]{:S(2)}) copy-start(bf16[64,320]{1,0:T(8,128)(2,1)} %param.18) | copy-start | bytes 122884
  221.7 171.9 %copy-start.4 = (f32[320]{0:T(512)S(1)}, f32[320]{0:T(512)}, u32[]{:S(2)}) copy-start(f32[320]{0:T(512)} %param.20) | copy-start | bytes 3844
  296.7 189.8 %all-reduce.7.cloned.1.call-start = ((), (), s32[]{:S(2)}) async-start(), calls=%async_computation.1 | async-start | bytes 3276800 | tf_op jit(solution)/shard_map/psum | solution.py:100
  393.5 5.3 %copy-start.5 = (u32[128]{0:T(128)S(1)}, u32[128]{0:T(128)}, u32[]{:S(2)}) copy-start(u32[128]{0:T(128)} %constant.51) | copy-start | bytes 1540
Sparse Core Ops, SparseCore 0:
  296.8 81.4 all-reduce.4
  399.0 87.4 all-reduce.6
